TPU v7x, 256 devices: a whole 4x4x8 slice. The times are simulated.
256 devices in a mesh: row: 8 (over z), col: 16 (over y, x), smp: 2 (over core).
Axes of the slice: x: 4, y: 4, z: 8, core: 2. Of those that a mesh axis runs over, the one named last changes fastest.
Arguments:
- state: float32 [8, 2048, 512], P('smp', ('row', 'col')), may hold values from -6 to 6
- noise: float32 [2, 8, 2048, 512], P(None, 'smp', ('row', 'col')), may hold values from -6 to 6
- pair: bfloat16 [2048, 2048, 128], P('row', 'col'), may hold values from -10 to 10
- contacts: int32 [16, 6], replicated, may hold values from -1 to 15, as said below
- norm_gain: float32 [512], replicated, may hold values from 0.1 to 1.9
- w_qkv: bfloat16 [512, 1536], replicated, may hold values from -0.25 to 0.25
- w_out: bfloat16 [512, 512], replicated, may hold values from -0.25 to 0.25
- w_bias: bfloat16 [128, 32], replicated, may hold values from -1.5 to 1.5
Outputs:
- denoised: float32 [8, 2048, 512], P('smp', ('row', 'col'))
Inputs may be any that keep to these rules, and one draw needn't show every extreme that they name: `contacts`: row q lists distinct blocks, q itself first, then nearby blocks more often than far ones; its first counts are blocks and the remaining slots hold -1; some row uses all 6 slots.
All inputs are finite; a program needn't handle non-finite values.
Results may differ from a plain program's by a relative error of at most 0.012.
Values may be sent and summed in bfloat16 or wider, within the bound.
A program may use at most 128 MiB of HBM per device.

v0:
```python
import jax
import jax.numpy as jnp
from jax import lax
from jax.sharding import PartitionSpec as P

STEPS = 2


def from_root(block, axis, owner):
    block = jnp.where(lax.axis_index(axis) == owner, block, jnp.zeros_like(block))
    return lax.psum(block, axis)


def body(state, noise, pair, contacts, norm_gain, w_qkv, w_out, w_bias):
    samples_dev, rows_dev, width = state.shape
    heads = w_bias.shape[1]
    head_dim = width // heads
    row_span, blk = (pair.shape[0], pair.shape[1])
    per_row = row_span // blk
    half = row_span // lax.axis_size("smp")
    own_rows = lax.dynamic_slice_in_dim(pair, lax.axis_index("smp") * half, half, 0)
    part_bias = jnp.einsum(
        "ijc,ch->hij", own_rows, w_bias, preferred_element_type=jnp.float32
    ).astype(jnp.bfloat16)
    bias = lax.all_gather(part_bias, "smp", axis=1, tiled=True).astype(jnp.float32)
    col_index = lax.axis_index("col")
    row_index = lax.axis_index("row")
    listed = lax.dynamic_slice_in_dim(contacts, row_index * per_row, per_row, 0)
    matched = jnp.any(listed == col_index, axis=1)
    allowed = jnp.repeat(matched, blk, total_repeat_length=row_span)
    busy = jnp.any(matched)
    x = state
    for step in range(STEPS):
        mean = jnp.mean(x, axis=-1, keepdims=True)
        var = jnp.mean((x - mean) ** 2, axis=-1, keepdims=True)
        normed = ((x - mean) * lax.rsqrt(var + 1e-05) * norm_gain).astype(jnp.bfloat16)
        qkv = jnp.dot(normed, w_qkv, preferred_element_type=jnp.float32).astype(jnp.bfloat16)
        block_rows = lax.all_gather(qkv, "col", axis=1, tiled=True)
        offset = col_index % per_row * blk
        mine = lax.dynamic_slice_in_dim(block_rows[..., width:], offset, blk, 1)
        keyval = from_root(mine, "row", col_index // per_row)
        queries = block_rows[..., :width].reshape(samples_dev, row_span, heads, head_dim)
        keys = keyval[..., :width].reshape(samples_dev, blk, heads, head_dim)
        values = keyval[..., width:].reshape(samples_dev, blk, heads, head_dim)

        def attend(unused):
            scores = (
                jnp.einsum("srhd,skhd->hsrk", queries, keys, preferred_element_type=jnp.float32)
                * 0.25
                + bias[:, None]
            )
            m_raw = jnp.max(scores, axis=-1)
            m_blk = jnp.where(allowed[None, None, :], m_raw, jnp.float32(-1e30))
            probs = jnp.where(
                allowed[None, None, :, None], jnp.exp(scores - m_raw[..., None]), jnp.float32(0.0)
            )
            totals = jnp.sum(probs, axis=-1)
            outputs = jnp.einsum(
                "hsrk,skhd->srhd",
                probs.astype(jnp.bfloat16),
                values,
                preferred_element_type=jnp.float32,
            )
            return (
                m_blk.transpose(1, 2, 0),
                totals.transpose(1, 2, 0),
                outputs.reshape(samples_dev, row_span, width),
            )

        def skipped(unused):
            return (
                jnp.full((samples_dev, row_span, heads), -1e30, jnp.float32),
                jnp.zeros((samples_dev, row_span, heads), jnp.float32),
                jnp.zeros((samples_dev, row_span, width), jnp.float32),
            )

        m_blk, totals, outputs = lax.cond(busy, attend, skipped, 0)
        top = lax.pmax(m_blk.astype(jnp.bfloat16), "col").astype(m_blk.dtype)
        weight = jnp.exp(m_blk - top)
        scaled = (
            outputs.reshape(samples_dev, row_span, heads, head_dim) * weight[..., None]
        ).reshape(samples_dev, row_span, width)
        summed, acc = (
            lax.psum_scatter(totals * weight, "col", scatter_dimension=1, tiled=True),
            lax.psum_scatter(scaled, "col", scatter_dimension=1, tiled=True),
        )
        attn = (acc.reshape(samples_dev, rows_dev, heads, head_dim) / summed[..., None]).reshape(
            samples_dev, rows_dev, width
        )
        attn = attn.astype(jnp.bfloat16)
        out = jnp.dot(attn, w_out, preferred_element_type=jnp.float32)
        x = x + out + 0.5 * 0.5**step * noise[step]
    return x


def solution(mesh):
    in_specs = (
        P("smp", ("row", "col"), None),
        P(None, "smp", ("row", "col"), None),
        P("row", "col", None),
        P(),
        P(),
        P(),
        P(),
        P(),
    )
    out_specs = P("smp", ("row", "col"), None)
    return jax.shard_map(body, mesh=mesh, in_specs=in_specs, out_specs=out_specs, check_vma=False)
```

profile of v0, /device:TPU:1, one launch (start us, length us, event | category | flops | bytes accessed | tf_op | source)
XLA Modules:
  0.0 770.3 jit_solution(14538606355737976069)
XLA Ops:
  6.5 1.1 reduce_sum.54
  7.7 1.1 multiply_reduce_fusion.1
  8.7 2.0 convolution_convert_fusion.1
  10.8 4.8 fusion.23
  15.7 51.2 %all-gather.4.cloned.1.call-done = bf16[4,256,1536]{2,1,0:T(8,128)(2,1)} async-done(((bf16[4,16,1536]{2,1,0:T(8,128)(2,1)}), bf16[4,256,1536]{2,1,0:T(8,128)(2,1)}) %all-gather.4.cloned.1.call-update) | async-done | bytes 3145744 | tf_op jit(solution)/shard_map/all_gather | solution.py:38
  66.9 1.6 slice-done
  68.5 1.2 dynamic-slice_select_fusion.1
  71.8 1.2 select_reduce_fusion
  73.0 11.8 %all-gather.6.cloned.1.call-done = bf16[32,256,128]{2,0,1:T(8,128)(2,1)} async-done(((bf16[32,128,128]{2,0,1:T(8,128)(2,1)}), bf16[32,256,128]{2,0,1:T(8,128)(2,1)}) %all-gather.6.cloned.1.call-update) | async-done | bytes 2097168 | tf_op jit(solution)/shard_map/all_gather | solution.py:25
  84.8 4.1 convert_element_type.54
  88.9 70.4 %all-reduce.13.cloned.1.call-done = bf16[4,128,1024]{2,1,0:T(8,128)(2,1)} async-done(((bf16[4,128,1024]{2,1,0:T(8,128)(2,1)}), bf16[4,128,1024]{2,1,0:T(8,128)(2,1)}) %all-reduce.13.cloned.1.call-update) | async-done | bytes 1048592 | tf_op jit(solution)/shard_map/psum | solution.py:11
  159.4 29.7 %conditional.2 = (f32[4,256,512]{1,2,0:T(8,128)}, f32[4,256,32]{1,2,0:T(8,128)}, f32[4,256,32]{1,2,0:T(8,128)}) conditional(s32[]{:T(128)} %convert_element_type.49, () %tuple.25, (pred[256]{0:T(512)(128)(4,1)S(1)}, bf16[4,256,1536]{2,1,0:T(8,128)(2,1)}, bf16[4,128,1024]{2,1,0:T(8,128)(2,1)}, f32[32,256,128]{2,0,1:T(8,128)}) %tuple.26), branch_computations={%region_5.6_spmd, %region_6.9_spmd} | conditional | flops 306151424 | bytes 102367824 | solution.py:77
  159.4 5.3 copy.95
  164.6 1.6 copy.94
  166.3 0.9 fusion.47
  167.1 4.6 copy.93
  171.8 1.3 slice.60
  173.1 5.4 fusion
  178.5 6.6 fusion.2
  186.5 2.6 fusion.3
  189.1 1.5 convert_element_type.55
  190.7 93.2 %all-reduce.15.cloned.1.call-done = bf16[4,256,32]{1,2,0:T(8,128)(2,1)} async-done(((bf16[4,256,32]{1,2,0:T(8,128)(2,1)}), bf16[4,256,32]{1,2,0:T(8,128)(2,1)}) %all-reduce.15.cloned.1.call-update) | async-done | bytes 65552 | tf_op jit(solution)/shard_map/pmax | solution.py:78
  283.9 1.0 fusion.46
  284.9 3.2 bitcast_multiply_fusion.1
  288.1 3.1 copy.98
  291.3 1.1 copy.100
  293.6 102.3 %all-reduce.23.cloned.1.call-done = (f32[4,256,32]{2,0,1:T(4,128)}, f32[4,256,512]{2,0,1:T(4,128)}) async-done(((f32[4,256,32]{2,0,1:T(4,128)}, f32[4,256,512]{2,0,1:T(4,128)}), (f32[4,256,32]{2,0,1:T(4,128)}, f32[4,256,512]{2,0,1:T(4,128)})) %all-reduce.23.cloned.1.call-update) | async-done | bytes 2228240
  396.7 1.6 constant_dynamic-slice_fusion.3
  399.3 1.3 fusion.50
  400.7 1.1 convolution_convert_fusion
  401.9 52.4 %all-gather.8.cloned.1.call-done = bf16[4,256,1536]{2,1,0:T(8,128)(2,1)} async-done(((bf16[4,16,1536]{2,1,0:T(8,128)(2,1)}), bf16[4,256,1536]{2,1,0:T(8,128)(2,1)}) %all-gather.8.cloned.1.call-update) | async-done | bytes 3145744 | tf_op jit(solution)/shard_map/all_gather | solution.py:38
  454.4 1.6 slice-done.1
  456.0 1.2 dynamic-slice_select_fusion
  457.3 71.1 %all-reduce.17.cloned.1.call-done = bf16[4,128,1024]{2,1,0:T(8,128)(2,1)} async-done(((bf16[4,128,1024]{2,1,0:T(8,128)(2,1)}), bf16[4,128,1024]{2,1,0:T(8,128)(2,1)}) %all-reduce.17.cloned.1.call-update) | async-done | bytes 1048592 | tf_op jit(solution)/shard_map/psum | solution.py:11
  528.4 25.1 %conditional.3 = (f32[4,256,512]{1,2,0:T(8,128)}, f32[4,256,32]{1,2,0:T(8,128)S(1)}, f32[4,256,32]{1,2,0:T(8,128)S(1)}) conditional(s32[]{:T(128)} %convert_element_type.49, () %tuple.27, (pred[256]{0:T(512)(128)(4,1)S(1)}, bf16[4,256,1536]{2,1,0:T(8,128)(2,1)}, bf16[4,128,1024]{2,1,0:T(8,128)(2,1)}, f32[32,256,128]{2,0,1:T(8,128)}) %tuple.28), branch_computations={%region_15.16_spmd, %region_16.19_spmd} | conditional | flops 306151424 | bytes 106037840 | solution.py:77
  528.4 5.4 copy.105
  534.5 4.6 copy.103
  539.1 1.3 slice.63
  540.5 4.5 fusion.8
  545.0 5.8 fusion.10
  550.9 2.6 fusion.11
  554.2 93.3 %all-reduce.19.cloned.1.call-done = bf16[4,256,32]{1,2,0:T(8,128)(2,1)} async-done(((bf16[4,256,32]{1,2,0:T(8,128)(2,1)}), bf16[4,256,32]{1,2,0:T(8,128)(2,1)}) %all-reduce.19.cloned.1.call-update) | async-done | bytes 65552 | tf_op jit(solution)/shard_map/pmax | solution.py:78
  648.4 3.1 bitcast_multiply_fusion
  651.5 3.2 copy.108
  654.7 1.0 copy.110
  655.7 103.6 %all-reduce.21.cloned.1.call-done = (f32[4,256,32]{2,0,1:T(4,128)}, f32[4,256,512]{2,0,1:T(4,128)}) async-done(((f32[4,256,32]{2,0,1:T(4,128)}, f32[4,256,512]{2,0,1:T(4,128)}), (f32[4,256,32]{2,0,1:T(4,128)}, f32[4,256,512]{2,0,1:T(4,128)})) %all-reduce.21.cloned.1.call-update) | async-done | bytes 2228240
  760.1 0.9 constant_dynamic-slice_fusion.1
  762.0 1.8 fusion.26
  (71 shorter events, 9.8 us)
Async XLA Ops:
  6.5 2.2 copy-start
  6.5 60.4 %all-gather.4.cloned.1.call-start = ((), (), s32[]{:S(2)}) async-start(), calls=%async_computation | async-start | bytes 3342336 | tf_op jit(solution)/shard_map/all_gather | solution.py:38
  10.8 74.0 %all-gather.6.cloned.1.call-start = ((), (), s32[]{:S(2)}) async-start(), calls=%async_computation.2 | async-start | bytes 3145728 | tf_op jit(solution)/shard_map/all_gather | solution.py:25
  15.6 54.2 %copy-start.9 = (s32[16,6]{0,1:T(8,128)S(1)}, s32[16,6]{0,1:T(8,128)}, u32[]{:S(2)}) copy-start(s32[16,6]{0,1:T(8,128)} %param.17) | copy-start | bytes 1156
  15.6 143.7 %all-reduce.13.cloned.1.call-start = ((), (), s32[]{:S(2)}) async-start(), calls=%async_computation.1 | async-start | bytes 2097152 | tf_op jit(solution)/shard_map/psum | solution.py:11
  66.9 1.6 slice-start
  69.7 214.2 %all-reduce.15.cloned.1.call-start = ((), (), s32[]{:S(2)}) async-start(), calls=%async_computation.3 | async-start | bytes 131072 | tf_op jit(solution)/shard_map/pmax | solution.py:78
  173.1 5.4 copy-start.2
  178.5 6.6 copy-start.6
  190.6 205.4 %all-reduce.23.cloned.1.call-start = ((), (), s32[]{:S(2)}) async-start(), calls=%async_computation.8 | async-start | bytes 5242880
  288.1 4.3 copy-start.10
  288.1 111.2 %copy-start.4 = (f32[4,16,512]{2,1,0:T(8,128)S(1)}, f32[4,16,512]{2,1,0:T(8,128)}, u32[]{:S(2)}) copy-start(f32[4,16,512]{2,1,0:T(8,128)} %param.14) | copy-start | bytes 393220
  288.1 111.2 %copy-start.5 = (bf16[512,512]{1,0:T(8,128)(2,1)S(1)}, bf16[512,512]{1,0:T(8,128)(2,1)}, u32[]{:S(2)}) copy-start(bf16[512,512]{1,0:T(8,128)(2,1)} %param.20) | copy-start | bytes 1572868
  291.2 109.5 %copy-start.8 = (f32[512]{0:T(512)S(1)}, f32[512]{0:T(512)}, u32[]{:S(2)}) copy-start(f32[512]{0:T(512)} %param.18) | copy-start | bytes 6148
  292.3 162.0 %all-gather.8.cloned.1.call-start = ((), (), s32[]{:S(2)}) async-start(), calls=%async_computation.4 | async-start | bytes 3342336 | tf_op jit(solution)/shard_map/all_gather | solution.py:38
  401.9 126.5 %all-reduce.17.cloned.1.call-start = ((), (), s32[]{:S(2)}) async-start(), calls=%async_computation.5 | async-start | bytes 2097152 | tf_op jit(solution)/shard_map/psum | solution.py:11
  454.4 1.6 slice-start.1
  457.2 190.3 %all-reduce.19.cloned.1.call-start = ((), (), s32[]{:S(2)}) async-start(), calls=%async_computation.6 | async-start | bytes 131072 | tf_op jit(solution)/shard_map/pmax | solution.py:78
  528.4 5.4 copy-start.7
  540.4 4.5 copy-start.3
  554.2 205.2 %all-reduce.21.cloned.1.call-start = ((), (), s32[]{:S(2)}) async-start(), calls=%async_computation.7 | async-start | bytes 5242880
  651.5 112.3 %copy-start.1 = (bf16[512,1536]{1,0:T(8,128)(2,1)S(1)}, bf16[512,1536]{1,0:T(8,128)(2,1)}, u32[]{:S(2)}) copy-start(bf16[512,1536]{1,0:T(8,128)(2,1)} %param.19) | copy-start | bytes 4718596
Sparse Core Ops, SparseCore 0:
  10.9 55.9 all-gather.3
  68.7 16.0 all-gather.5
  87.2 72.1 all-reduce.12
  190.7 93.1 all-reduce.14
  292.5 103.4 all-reduce.22
  402.0 52.3 all-gather.7
  457.3 71.0 all-reduce.16
  554.3 93.1 all-reduce.18
  655.8 103.4 all-reduce.20
where the time goes:
time: 771 us; the launch traced here: 770 us
  waiting for transfers between devices  650 us (84%)
  local copies, waits for them, and re-layouts  45.9 us (6%)
  other arithmetic  33.8 us (4%)
  matrix products  26 us (3%)
  between operations  14.7 us (2%)
    unnamed x11, waiting for transfers between devices  206 us
    pmax x2, waiting for transfers between devices, body(): top = lax.pmax(m_blk.astype(jnp.bfloat16), 'col').astype(m_blk.dtype)  187 us
    psum x2, waiting for transfers between devices, from_root(): return lax.psum(block, axis)  142 us
    all_gather x2, waiting for transfers between devices, body(): block_rows = lax.all_gather(qkv, 'col', axis=1, tiled=True)  104 us
    another operation x6, local copies, waits for them, and re-layouts  22.2 us
  transfers between devices with their start and end apart: 9, of which 9 were waited for; matrix products, arithmetic and copies ran while one was open for 2% of the time, Pallas kernels for 0%

commit v1 on v0

--- a/solution.py
+++ b/solution.py
@@ -35,7 +35,9 @@
         var = jnp.mean((x - mean) ** 2, axis=-1, keepdims=True)
         normed = ((x - mean) * lax.rsqrt(var + 1e-05) * norm_gain).astype(jnp.bfloat16)
         qkv = jnp.dot(normed, w_qkv, preferred_element_type=jnp.float32).astype(jnp.bfloat16)
-        block_rows = lax.all_gather(qkv, "col", axis=1, tiled=True)
+        block_rows = jnp.concatenate(
+            lax.all_to_all(jnp.stack([qkv] * lax.axis_size("col")), "col", 0, 0), axis=1
+        )
         offset = col_index % per_row * blk
         mine = lax.dynamic_slice_in_dim(block_rows[..., width:], offset, blk, 1)
         keyval = from_root(mine, "row", col_index // per_row)

time: 771 us -> 747 us (0.969)
  waiting for transfers between devices: 650 us -> 569 us
  blocking collectives: 0 us -> 42.6 us
    all_gather x2 -> x0, waiting for transfers between devices: 104 us -> none  [body(): block_rows = lax.all_gather(qkv, 'col', axis=1, tiled=True)]
    all_to_all x0 -> x1, blocking collectives: none -> 42.6 us  [body(): lax.all_to_all(jnp.stack([qkv] * lax.axis_size('col')), 'col', 0, 0)]
    all_to_all x0 -> x1, waiting for transfers between devices: none -> 42 us  [body(): lax.all_to_all(jnp.stack([qkv] * lax.axis_size('col')), 'col', 0, 0)]
    all_gather x1, waiting for transfers between devices: 11.8 us -> 0.02 us  [body(): lax.all_gather(part_bias, 'smp', axis=1, tiled=True).astype(jnp.float32)]
    another operation x6 -> x8, local copies, waits for them, and re-layouts: 22.2 us -> 24.6 us
    unnamed x11 -> x9, waiting for transfers between devices: 206 us -> 205 us
  transfers between devices with their start and end apart: 9 -> 8, of which waited for: 9 -> 7; matrix products, arithmetic and copies ran while one was open for 2% -> 2% of each run, Pallas kernels for 0% -> 0%
where the time goes in v1:
time: 747 us; the launch traced here: 746 us
  waiting for transfers between devices  569 us (76%)
  local copies, waits for them, and re-layouts  51.5 us (7%)
  blocking collectives  42.6 us (6%)
  other arithmetic  33.8 us (5%)
  matrix products  24.5 us (3%)
  between operations  16.5 us (2%)
  starting transfers between devices  7.92 us (1%)
    unnamed x9, waiting for transfers between devices  205 us
    pmax x2, waiting for transfers between devices, body(): top = lax.pmax(m_blk.astype(jnp.bfloat16), 'col').astype(m_blk.dtype)  186 us
    psum x2, waiting for transfers between devices, from_root(): return lax.psum(block, axis)  136 us
    all_to_all x1, blocking collectives, body(): lax.all_to_all(jnp.stack([qkv] * lax.axis_size('col')), 'col', 0, 0)  42.6 us
    all_to_all x1, waiting for transfers between devices, body(): lax.all_to_all(jnp.stack([qkv] * lax.axis_size('col')), 'col', 0, 0)  42 us
    another operation x6, local copies, waits for them, and re-layouts  22.2 us
  transfers between devices with their start and end apart: 8, of which 7 were waited for; matrix products, arithmetic and copies ran while one was open for 2% of the time, Pallas kernels for 0%

profile of v1, /device:TPU:1, one launch (start us, length us, event | category | flops | bytes accessed | tf_op | source)
XLA Modules:
  0.0 746.0 jit_solution(9172947712839519341)
XLA Ops:
  7.4 1.1 reduce_sum.54
  8.5 1.1 multiply_reduce_fusion.1
  9.6 1.3 convolution_convert_fusion.1
  10.9 2.1 stack.4
  13.0 7.6 %all-to-all-start = ((bf16[16,4,16,1536]{3,2,1,0:T(8,128)(2,1)}), bf16[16,4,16,1536]{3,2,1,0:T(8,128)(2,1)}, u32[]{:S(2)}, u32[]{:S(2)}) async-start(bf16[16,4,16,1536]{3,2,1,0:T(8,128)(2,1)} %stack.4), calls=%async_computation | async-start | bytes 6291456 | tf_op jit(solution)/shard_map/all_to_all | solution.py:39
  20.7 4.7 fusion.23
  25.5 42.0 %all-to-all-done = bf16[16,4,16,1536]{3,2,1,0:T(8,128)(2,1)} async-done(((bf16[16,4,16,1536]{3,2,1,0:T(8,128)(2,1)}), bf16[16,4,16,1536]{3,2,1,0:T(8,128)(2,1)}, u32[]{:S(2)}, u32[]{:S(2)}) %all-to-all-start) | async-done | bytes 3145760 | tf_op jit(solution)/shard_map/all_to_all | solution.py:39
  67.5 2.1 copy.98
  69.7 1.7 copy-done.4
  71.7 1.2 dynamic-slice_select_fusion.1
  75.0 1.3 select_reduce_fusion
  76.3 4.1 convert_element_type.54
  80.4 65.2 %all-reduce.13.cloned.1.call-done = bf16[4,128,1024]{2,1,0:T(8,128)(2,1)} async-done(((bf16[4,128,1024]{2,1,0:T(8,128)(2,1)}), bf16[4,128,1024]{2,1,0:T(8,128)(2,1)}) %all-reduce.13.cloned.1.call-update) | async-done | bytes 1048592 | tf_op jit(solution)/shard_map/psum | solution.py:11
  145.6 29.6 %conditional.2 = (f32[4,256,512]{1,2,0:T(8,128)}, f32[4,256,32]{1,2,0:T(8,128)}, f32[4,256,32]{1,2,0:T(8,128)}) conditional(s32[]{:T(128)} %convert_element_type.49, () %tuple.25, (pred[256]{0:T(512)(128)(4,1)S(1)}, bf16[4,256,1536]{2,1,0:T(8,128)(2,1)}, bf16[4,128,1024]{2,1,0:T(8,128)(2,1)}, f32[32,256,128]{2,0,1:T(8,128)}) %tuple.78), branch_computations={%region_5.6_spmd, %region_6.9_spmd} | conditional | flops 306151424 | bytes 102367824 | solution.py:79
  145.6 5.3 copy.101
  150.9 1.6 copy.100
  153.4 4.6 copy.99
  158.0 1.3 slice.60
  159.3 5.3 fusion
  164.6 6.6 fusion.2
  172.6 2.5 fusion.3
  175.2 1.5 convert_element_type.55
  176.8 93.1 %all-reduce.15.cloned.1.call-done = bf16[4,256,32]{1,2,0:T(8,128)(2,1)} async-done(((bf16[4,256,32]{1,2,0:T(8,128)(2,1)}), bf16[4,256,32]{1,2,0:T(8,128)(2,1)}) %all-reduce.15.cloned.1.call-update) | async-done | bytes 65552 | tf_op jit(solution)/shard_map/pmax | solution.py:80
  269.9 1.0 fusion.46
  270.9 3.2 bitcast_multiply_fusion.1
  274.1 3.1 copy.104
  277.2 1.0 copy.106
  279.6 101.9 %all-reduce.23.cloned.1.call-done = (f32[4,256,32]{2,0,1:T(4,128)}, f32[4,256,512]{2,0,1:T(4,128)}) async-done(((f32[4,256,32]{2,0,1:T(4,128)}, f32[4,256,512]{2,0,1:T(4,128)}), (f32[4,256,32]{2,0,1:T(4,128)}, f32[4,256,512]{2,0,1:T(4,128)})) %all-reduce.23.cloned.1.call-update) | async-done | bytes 2228240
  382.3 1.6 constant_dynamic-slice_fusion.3
  384.8 1.3 fusion.50
  387.1 42.6 %all_to_all.10 = bf16[16,4,16,1536]{3,2,1,0:T(8,128)(2,1)S(1)} all-to-all(bf16[16,4,16,1536]{3,2,1,0:T(8,128)(2,1)S(1)} %stack.5), channel_id=1, replica_groups=mesh['row'=8,'col'=16,'smp'=2] {'col'}, dimensions={0} | all-to-all | bytes 6291456 | tf_op jit(solution)/shard_map/all_to_all | solution.py:39
  430.0 1.7 copy-done.5
  432.0 1.2 dynamic-slice_select_fusion
  433.3 70.5 %all-reduce.17.cloned.1.call-done = bf16[4,128,1024]{2,1,0:T(8,128)(2,1)} async-done(((bf16[4,128,1024]{2,1,0:T(8,128)(2,1)}), bf16[4,128,1024]{2,1,0:T(8,128)(2,1)}) %all-reduce.17.cloned.1.call-update) | async-done | bytes 1048592 | tf_op jit(solution)/shard_map/psum | solution.py:11
  503.8 25.1 %conditional.3 = (f32[4,256,512]{1,2,0:T(8,128)}, f32[4,256,32]{1,2,0:T(8,128)S(1)}, f32[4,256,32]{1,2,0:T(8,128)S(1)}) conditional(s32[]{:T(128)} %convert_element_type.49, () %tuple.27, (pred[256]{0:T(512)(128)(4,1)S(1)}, bf16[4,256,1536]{2,1,0:T(8,128)(2,1)}, bf16[4,128,1024]{2,1,0:T(8,128)(2,1)}, f32[32,256,128]{2,0,1:T(8,128)}) %tuple.79), branch_computations={%region_15.16_spmd, %region_16.19_spmd} | conditional | flops 306151424 | bytes 106037840 | solution.py:79
  503.8 5.4 copy.112
  509.9 4.6 copy.110
  514.5 1.3 slice.63
  515.8 4.5 fusion.8
  520.4 5.8 fusion.10
  526.3 2.6 fusion.11
  529.6 93.1 %all-reduce.19.cloned.1.call-done = bf16[4,256,32]{1,2,0:T(8,128)(2,1)} async-done(((bf16[4,256,32]{1,2,0:T(8,128)(2,1)}), bf16[4,256,32]{1,2,0:T(8,128)(2,1)}) %all-reduce.19.cloned.1.call-update) | async-done | bytes 65552 | tf_op jit(solution)/shard_map/pmax | solution.py:80
  623.5 3.1 bitcast_multiply_fusion
  626.6 3.2 copy.115
  629.8 1.0 copy.117
  630.9 103.2 %all-reduce.21.cloned.1.call-done = (f32[4,256,32]{2,0,1:T(4,128)}, f32[4,256,512]{2,0,1:T(4,128)}) async-done(((f32[4,256,32]{2,0,1:T(4,128)}, f32[4,256,512]{2,0,1:T(4,128)}), (f32[4,256,32]{2,0,1:T(4,128)}, f32[4,256,512]{2,0,1:T(4,128)})) %all-reduce.21.cloned.1.call-update) | async-done | bytes 2228240
  734.9 0.9 constant_dynamic-slice_fusion.1
  736.8 1.8 fusion.26
  (76 shorter events, 12.3 us)
Async XLA Ops:
  7.4 2.2 copy-start
  10.9 9.8 %copy-start.10 = (bf16[128,32]{0,1:T(8,128)(2,1)S(1)}, bf16[128,32]{0,1:T(8,128)(2,1)}, u32[]{:S(2)}) copy-start(bf16[128,32]{0,1:T(8,128)(2,1)} %param.21) | copy-start | bytes 24580
  13.0 54.5 %all-to-all-start = ((bf16[16,4,16,1536]{3,2,1,0:T(8,128)(2,1)}), bf16[16,4,16,1536]{3,2,1,0:T(8,128)(2,1)}, u32[]{:S(2)}, u32[]{:S(2)}) async-start(bf16[16,4,16,1536]{3,2,1,0:T(8,128)(2,1)} %stack.4), calls=%async_computation | async-start | bytes 6291456 | tf_op jit(solution)/shard_map/all_to_all | solution.py:39
  20.6 55.7 %all-gather.2.cloned.1.call-start = ((), (), s32[]{:S(2)}) async-start(), calls=%async_computation.3 | async-start | bytes 3145728 | tf_op jit(solution)/shard_map/all_gather | solution.py:25
  25.4 120.2 %all-reduce.13.cloned.1.call-start = ((), (), s32[]{:S(2)}) async-start(), calls=%async_computation.2 | async-start | bytes 2097152 | tf_op jit(solution)/shard_map/psum | solution.py:11
  69.7 1.7 copy-start.4
  69.7 3.3 copy-start.12
  72.9 196.9 %all-reduce.15.cloned.1.call-start = ((), (), s32[]{:S(2)}) async-start(), calls=%async_computation.4 | async-start | bytes 131072 | tf_op jit(solution)/shard_map/pmax | solution.py:80
  159.3 5.4 copy-start.2
  164.6 6.6 copy-start.8
  176.7 204.8 %all-reduce.23.cloned.1.call-start = ((), (), s32[]{:S(2)}) async-start(), calls=%async_computation.8 | async-start | bytes 5242880
  274.1 4.3 copy-start.13
  274.1 110.7 %copy-start.6 = (f32[4,16,512]{2,1,0:T(8,128)S(1)}, f32[4,16,512]{2,1,0:T(8,128)}, u32[]{:S(2)}) copy-start(f32[4,16,512]{2,1,0:T(8,128)} %param.14) | copy-start | bytes 393220
  274.1 110.7 %copy-start.7 = (bf16[512,512]{1,0:T(8,128)(2,1)S(1)}, bf16[512,512]{1,0:T(8,128)(2,1)}, u32[]{:S(2)}) copy-start(bf16[512,512]{1,0:T(8,128)(2,1)} %param.20) | copy-start | bytes 1572868
  277.2 109.0 %copy-start.11 = (f32[512]{0:T(512)S(1)}, f32[512]{0:T(512)}, u32[]{:S(2)}) copy-start(f32[512]{0:T(512)} %param.18) | copy-start | bytes 6148
  278.3 225.5 %all-reduce.17.cloned.1.call-start = ((), (), s32[]{:S(2)}) async-start(), calls=%async_computation.5 | async-start | bytes 2097152 | tf_op jit(solution)/shard_map/psum | solution.py:11
  430.0 1.7 copy-start.5
  433.2 189.4 %all-reduce.19.cloned.1.call-start = ((), (), s32[]{:S(2)}) async-start(), calls=%async_computation.6 | async-start | bytes 131072 | tf_op jit(solution)/shard_map/pmax | solution.py:80
  503.8 5.4 copy-start.9
  515.8 4.6 copy-start.3
  529.5 204.6 %all-reduce.21.cloned.1.call-start = ((), (), s32[]{:S(2)}) async-start(), calls=%async_computation.7 | async-start | bytes 5242880
  626.6 111.9 %copy-start.1 = (bf16[512,1536]{1,0:T(8,128)(2,1)S(1)}, bf16[512,1536]{1,0:T(8,128)(2,1)}, u32[]{:S(2)}) copy-start(bf16[512,1536]{1,0:T(8,128)(2,1)} %param.19) | copy-start | bytes 4718596
Sparse Core Ops, SparseCore 0:
  25.5 20.0 all-gather.1
Sparse Core Ops, SparseCore 1:
  73.0 72.5 all-reduce.12
  176.8 93.0 all-reduce.14
  278.4 103.1 all-reduce.22
  433.3 70.4 all-reduce.16
  529.6 93.0 all-reduce.18
  631.0 103.1 all-reduce.20
